TPU v7x, 512 devices: a whole 4x8x8 slice. The times are simulated.
512 devices in a mesh: row: 16 (over y, core), col: 32 (over z, x).
Axes of the slice: x: 4, y: 8, z: 8, core: 2. Of those that a mesh axis runs over, the one named last changes fastest.
Arguments:
- grad_out: bfloat16 [2048, 8192], P('col', 'row'), may hold values from -0.09375 to 0.09375
- activations: bfloat16 [2048, 28672], P('row', 'col'), may hold values from -6 to 6
- left_steps: float32 [10, 8192], P(None, 'row')
- left_curves: float32 [10, 8192], P(None, 'row'), as said below
- right_steps: float32 [10, 28672], P(None, 'col')
- right_curves: float32 [10, 28672], P(None, 'col'), as said below
Outputs:
- direction: float32 [8192, 28672], P('row', 'col')
Inputs may be any that keep to these rules, and one draw needn't show every extreme that they name: `left_curves`: each curve row is its step row scaled entrywise by positive factors, so every step has a positive inner product with its curve; the last pair is the newest. `right_curves`: as for the output side.
All inputs are finite; a program needn't handle non-finite values.
Results may differ from a plain program's by a relative error of at most 0.0003.
Values may be sent and summed in bfloat16 or wider, within the bound.
No kernel may reach another device: no remote copies, remote signals or barrier semaphores. Data moves between devices by JAX's collectives and lax.ppermute only.
A program may use at most 64 MiB of HBM per device.

v0:
```python
import jax
import jax.numpy as jnp
from jax import lax
from jax.sharding import PartitionSpec as P

HIGH = lax.Precision.HIGHEST


def upper_inverse(upper_tri):
    count = upper_tri.shape[0]
    identity = jnp.eye(count, dtype=upper_tri.dtype)
    inv_rows = [None] * count
    for index in reversed(range(count)):
        running = identity[index]
        for later in range(index + 1, count):
            running = running - upper_tri[index, later] * inv_rows[later]
        inv_rows[index] = running / upper_tri[index, index]
    return jnp.stack(inv_rows, 0)


def compact(pair_sy, pair_yy):
    scaling = pair_sy[-1, -1] / pair_yy[-1, -1]
    upper_tri = jnp.triu(pair_sy)
    inverse = upper_inverse(upper_tri)
    middle = jnp.diag(jnp.diag(pair_sy)) + scaling * pair_yy
    return (scaling, inverse, middle)


def pair_products(step_rows, curv_rows):
    pair_sy = jnp.dot(step_rows, curv_rows.T, precision=HIGH, preferred_element_type=jnp.float32)
    pair_yy = jnp.dot(curv_rows, curv_rows.T, precision=HIGH, preferred_element_type=jnp.float32)
    return (pair_sy, pair_yy)


def apply_left(grad_block, step_rows, curv_rows, terms, proj_steps, proj_curves):
    scaling, inverse, middle = terms
    weighted = jnp.dot(inverse, proj_steps, precision=HIGH)
    coeffs = jnp.dot(
        inverse.T, jnp.dot(middle, weighted, precision=HIGH) - scaling * proj_curves, precision=HIGH
    )
    lefted = (
        scaling * grad_block
        + jnp.dot(step_rows.T, coeffs, precision=HIGH)
        - scaling * jnp.dot(curv_rows.T, weighted, precision=HIGH)
    )
    return (lefted, weighted, coeffs)


def apply_right(lefted, step_rows, curv_rows, terms, side_steps, side_curves):
    scaling, inverse, middle = terms
    weighted = jnp.dot(side_steps, inverse.T, precision=HIGH)
    coeffs = jnp.dot(
        jnp.dot(weighted, middle, precision=HIGH) - scaling * side_curves, inverse, precision=HIGH
    )
    return (
        scaling * lefted
        + jnp.dot(coeffs, step_rows, precision=HIGH)
        - scaling * jnp.dot(weighted, curv_rows, precision=HIGH)
    )


def on_device(grad_out, activations, left_steps, left_curves, right_steps, right_curves):
    contract = (((0,), (0,)), ((), ()))
    left_sy, left_yy = pair_products(left_steps, left_curves)
    right_sy, right_yy = pair_products(right_steps, right_curves)
    token_panel = lax.all_gather(activations, "row", axis=0, tiled=True)
    grad_block = lax.dot_general(
        lax.all_gather(grad_out, "col", axis=0, tiled=True),
        token_panel,
        contract,
        preferred_element_type=jnp.float32,
    )
    left_sy, left_yy = lax.psum((left_sy, left_yy), "row")
    right_sy, right_yy = lax.psum((right_sy, right_yy), "col")
    proj_steps, proj_curves = lax.psum(
        (
            jnp.dot(left_steps, grad_block, precision=HIGH),
            jnp.dot(left_curves, grad_block, precision=HIGH),
        ),
        "row",
    )
    lefted = apply_left(
        grad_block, left_steps, left_curves, compact(left_sy, left_yy), proj_steps, proj_curves
    )[0]
    side_steps, side_curves = lax.psum(
        (
            jnp.dot(lefted, right_steps.T, precision=HIGH),
            jnp.dot(lefted, right_curves.T, precision=HIGH),
        ),
        "col",
    )
    return apply_right(
        lefted, right_steps, right_curves, compact(right_sy, right_yy), side_steps, side_curves
    )


def solution(mesh):
    in_specs = (
        P("col", "row"),
        P("row", "col"),
        P(None, "row"),
        P(None, "row"),
        P(None, "col"),
        P(None, "col"),
    )
    out_specs = P("row", "col")
    return jax.shard_map(
        on_device, mesh=mesh, in_specs=in_specs, out_specs=out_specs, check_vma=False
    )
```

profile of v0, /device:TPU:8, one launch (start us, length us, event | category | flops | bytes accessed | tf_op | source)
XLA Modules:
  0.0 520.0 jit_solution(11072346568217692992)
XLA Ops:
  6.5 0.7 all-gather.3.cloned.1.call-update
  7.3 0.0 all-gather.5.cloned.1.call-start
  7.3 0.7 all-gather.5.cloned.1.call-update
  8.0 0.0 all-reduce.4.cloned.1.call-start
  8.1 1.6 fusion.26
  9.7 1.5 fusion.25
  11.2 0.2 fusion.24
  11.4 1.0 fusion.23
  12.4 0.0 copy-start.2
  12.5 86.7 %all-gather.3.cloned.1.call-done = bf16[2048,512]{1,0:T(8,128)(2,1)} async-done(((bf16[64,512]{1,0:T(8,128)(2,1)}), bf16[2048,512]{1,0:T(8,128)(2,1)}) %all-gather.3.cloned.1.call-update) | async-done | bytes 2097168 | tf_op jit(solution)/shard_map/all_gather | solution.py:68
  99.1 42.5 %all-gather.5.cloned.1.call-done = bf16[2048,896]{1,0:T(8,128)(2,1)} async-done(((bf16[128,896]{1,0:T(8,128)(2,1)}), bf16[2048,896]{1,0:T(8,128)(2,1)}) %all-gather.5.cloned.1.call-update) | async-done | bytes 3670032 | tf_op jit(solution)/shard_map/all_gather | solution.py:66
  141.6 5.0 fusion.27
  146.7 0.0 copy-start.1
  146.7 0.0 copy-start.4
  146.7 1.7 convolution_bitcast_fusion.1
  148.4 3.8 convolution_bitcast_fusion
  152.2 0.0 all-reduce.4.cloned.1.call-update
  152.2 112.5 %all-reduce.4.cloned.1.call-done = (f32[10,10]{1,0:T(8,128)}, f32[10,896]{0,1:T(8,128)}, f32[10,896]{1,0:T(8,128)}, f32[10,10]{1,0:T(8,128)}) async-done(((f32[10,10]{1,0:T(8,128)}, f32[10,896]{0,1:T(8,128)}, f32[10,896]{1,0:T(8,128)}, f32[10,10]{1,0:T(8,128)}), (f32[10,10]{1,0:T(8,128)}, f32[10,896]{0,1:T(8,128)}, f32[10,896]{1,0:T(8,128)}, f32[10,10]{1,0:T(8,128)})) %all-reduce.4.cloned.1.call-update) | async-done | bytes 72496 | tf_op jit(solution)/shard_map/psum | solution.py:73
  264.7 1.3 slice.532
  266.0 0.8 fusion.7
  266.8 0.7 fusion.22
  267.5 0.7 fusion.21
  268.2 0.7 fusion.20
  269.0 1.3 slice.533
  270.3 1.4 gather_fusion
  273.1 34.2 %subtract_divide_fusion.9 = (f32[1,10]{1,0:T(1,128)S(1)}, f32[1,10]{1,0:T(1,128)S(1)}, f32[1,10]{1,0:T(1,128)S(1)}, f32[1,10]{1,0:T(1,128)S(1)}, f32[1,10]{1,0:T...) fusion(f32[10,10]{1,0:T(8,128)S(1)} %fusion.8, ...), kind=kLoop, calls=%fused_computation.36 | loop fusion | flops 1000 | bytes 1020 | tf_op jit(solution)/shard_map/div | solution.py:17
  307.3 1.5 fusion.28
  308.9 1.1 convolution_subtract_fusion.1
  310.0 0.2 fusion.29
  310.2 1.6 fusion.30
  311.9 3.2 bitcast_subtract_fusion
  315.1 0.0 copy-start.3
  315.1 1.6 fusion.33
  316.7 1.8 fusion.31
  318.5 149.2 %all-reduce = (f32[512,10]{1,0:T(8,128)S(1)}, f32[10,10]{1,0:T(8,128)S(1)}, f32[512,10]{1,0:T(8,128)S(1)}, f32[10,10]{1,0:T(8,128)S(1)}) all-reduce(f32[512,10]{1,0:T(8,128)S(1)} %fusion.31, f32[10,10]{1,0:T(8,128)S(1)} %fusion.23, f32[512,10]{1,0:T(8,128)S(1)} %fusion.33, ...), channel_id=1, replica_groups=mesh['row'=16,'col'=32] {'col'}, use_global_device_ids=true, to_apply=%region_6.7 | all-reduce | flops 10440 | bytes 83520 | tf_op jit(solution)/shard_map/psum | solution.py:85
  467.7 0.6 slice.530
  468.3 0.7 gather_fusion.1
  469.0 0.1 fusion.6
  469.1 0.7 fusion.19
  469.8 0.7 fusion.18
  470.5 0.7 fusion.17
  471.3 0.6 slice.531
  473.2 34.4 %subtract_divide_fusion = (f32[1,10]{1,0:T(1,128)S(1)}, f32[1,10]{1,0:T(1,128)S(1)}, f32[1,10]{1,0:T(1,128)S(1)}, f32[1,10]{1,0:T(1,128)S(1)}, f32[1,10]{1,0:T(1...) fusion(f32[10,10]{1,0:T(8,128)S(1)} %fusion.8, ...), kind=kLoop, calls=%fused_computation.27 | loop fusion | flops 1000 | bytes 1020 | tf_op jit(solution)/shard_map/div | solution.py:17
  507.6 0.3 fusion.32
  507.9 0.6 convolution_subtract_fusion
  508.6 0.3 fusion.34
  508.9 1.6 fusion.35
  510.5 3.0 multiply_subtract_fusion
  (12 shorter events, 0.1 us)
Async XLA Ops:
  6.5 4.7 copy-start
  6.5 92.6 %all-gather.3.cloned.1.call-start = ((), (), s32[]{:S(2)}) async-start(), calls=%async_computation | async-start | bytes 2162688 | tf_op jit(solution)/shard_map/all_gather | solution.py:68
  7.3 134.4 %all-gather.5.cloned.1.call-start = ((), (), s32[]{:S(2)}) async-start(), calls=%async_computation.1 | async-start | bytes 3899392 | tf_op jit(solution)/shard_map/all_gather | solution.py:66
  8.0 256.7 %all-reduce.4.cloned.1.call-start = ((), (), s32[]{:S(2)}) async-start(), calls=%async_computation.2 | async-start | bytes 1064960 | tf_op jit(solution)/shard_map/psum | solution.py:73
  12.4 134.2 %copy-start.2 = (f32[10,512]{1,0:T(8,128)S(1)}, f32[10,512]{1,0:T(8,128)}, u32[]{:S(2)}) copy-start(f32[10,512]{1,0:T(8,128)} %param.9) | copy-start | bytes 61444
  146.7 1.7 copy-start.1
  146.7 1.7 copy-start.4
  315.1 1.6 copy-start.3
Sparse Core Ops, SparseCore 0:
  10.5 88.6 all-gather.2
  101.3 40.3 all-gather.4
  152.3 112.3 all-reduce.3
where the time goes:
time: 522 us; the launch traced here: 520 us
  waiting for transfers between devices  243 us (47%)
  blocking collectives  149 us (29%)
  other arithmetic  69.5 us (13%)
  matrix products  31.9 us (6%)
  between operations  15.9 us (3%)
  local copies, waits for them, and re-layouts  10.4 us (2%)
    psum x1, blocking collectives, on_device(): lax.psum((jnp.dot(lefted, right_steps.T, precision=HIGH), jnp.dot(lefted,...  149 us
    psum x1, waiting for transfers between devices, on_device(): left_sy, left_yy = lax.psum((left_sy, left_yy), 'row')  113 us
    all_gather x1, waiting for transfers between devices, on_device(): lax.all_gather(grad_out, 'col', axis=0, tiled=True)  86.7 us
    div x2, other arithmetic, upper_inverse(): inv_rows[index] = running / upper_tri[index, index]  68.6 us
    all_gather x1, waiting for transfers between devices, on_device(): token_panel = lax.all_gather(activations, 'row', axis=0, tiled=True)  42.5 us
  transfers between devices with their start and end apart: 3, of which 3 were waited for; matrix products, arithmetic and copies ran while one was open for 1% of the time, Pallas kernels for 0%

commit v1 on v0

--- a/solution.py
+++ b/solution.py
@@ -4,6 +4,27 @@
 from jax.sharding import PartitionSpec as P
 
 HIGH = lax.Precision.HIGHEST
+
+
+def gather_around(x, axis, dim):
+    devices, mine, span = (lax.axis_size(axis), lax.axis_index(axis), x.shape[dim])
+    right = [(i, (i + 1) % devices) for i in range(devices)]
+    behind = [(i, (i - 1) % devices) for i in range(devices)]
+    filled = jnp.zeros((*x.shape[:dim], devices * span, *x.shape[dim + 1 :]), x.dtype)
+    filled = lax.dynamic_update_slice_in_dim(filled, x, mine * span, axis=dim)
+    from_left = from_right = x
+    halfway = devices // 2
+    for hop in range(1, halfway + 1):
+        from_left = lax.ppermute(from_left, axis, right)
+        filled = lax.dynamic_update_slice_in_dim(
+            filled, from_left, (mine - hop) % devices * span, axis=dim
+        )
+        if hop < devices - halfway:
+            from_right = lax.ppermute(from_right, axis, behind)
+            filled = lax.dynamic_update_slice_in_dim(
+                filled, from_right, (mine + hop) % devices * span, axis=dim
+            )
+    return filled
 
 
 def upper_inverse(upper_tri):
@@ -63,7 +84,7 @@
     contract = (((0,), (0,)), ((), ()))
     left_sy, left_yy = pair_products(left_steps, left_curves)
     right_sy, right_yy = pair_products(right_steps, right_curves)
-    token_panel = lax.all_gather(activations, "row", axis=0, tiled=True)
+    token_panel = gather_around(activations, "row", 0)
     grad_block = lax.dot_general(
         lax.all_gather(grad_out, "col", axis=0, tiled=True),
         token_panel,

time: 522 us -> 480 us (0.920)
  waiting for transfers between devices: 243 us -> 169 us
  starting transfers between devices: 0.08 us -> 18.7 us
  local copies, waits for them, and re-layouts: 10.4 us -> 26.5 us
    all_gather x1, waiting for transfers between devices: 86.7 us -> 38.6 us  [on_device(): lax.all_gather(grad_out, 'col', axis=0, tiled=True)]
    all_gather x1 -> x0, waiting for transfers between devices: 42.5 us -> none  [on_device(): token_panel = lax.all_gather(activations, 'row', axis=0, tiled=True)]
    ppermute x0 -> x15, waiting for transfers between devices: none -> 19.2 us  [the longest x8 19.2 us: gather_around(): from_left = lax.ppermute(from_left, axis, right)]
    ppermute x0 -> x15, starting transfers between devices: none -> 18.6 us  [the longest x7 18.6 us: gather_around(): from_right = lax.ppermute(from_right, axis, behind)]
    dynamic_update_slice x0 -> x16, local copies, waits for them, and re-layouts: none -> 11.3 us  [the longest x8 5.66 us: gather_around(): lax.dynamic_update_slice_in_dim(filled, from_left, (mine - hop) % devices...]
  transfers between devices with their start and end apart: 3 -> 17, of which waited for: 3 -> 9; matrix products, arithmetic and copies ran while one was open for 1% -> 3% of each run, Pallas kernels for 0% -> 0%
where the time goes in v1:
time: 480 us; the launch traced here: 479 us
  waiting for transfers between devices  169 us (35%)
  blocking collectives  149 us (31%)
  other arithmetic  69.5 us (14%)
  matrix products  30.2 us (6%)
  local copies, waits for them, and re-layouts  26.5 us (6%)
  starting transfers between devices  18.7 us (4%)
  between operations  16.4 us (3%)
    psum x1, blocking collectives, on_device(): lax.psum((jnp.dot(lefted, right_steps.T, precision=HIGH), jnp.dot(lefted,...  149 us
    psum x1, waiting for transfers between devices, on_device(): left_sy, left_yy = lax.psum((left_sy, left_yy), 'row')  110 us
    div x2, other arithmetic, upper_inverse(): inv_rows[index] = running / upper_tri[index, index]  68.6 us
    all_gather x1, waiting for transfers between devices, on_device(): lax.all_gather(grad_out, 'col', axis=0, tiled=True)  38.6 us
    ppermute x8, waiting for transfers between devices, gather_around(): from_left = lax.ppermute(from_left, axis, right)  19.2 us
    ppermute x7, starting transfers between devices, gather_around(): from_right = lax.ppermute(from_right, axis, behind)  18.6 us
  transfers between devices with their start and end apart: 17, of which 9 were waited for; matrix products, arithmetic and copies ran while one was open for 3% of the time, Pallas kernels for 0%

profile of v1, /device:TPU:8, one launch (start us, length us, event | category | flops | bytes accessed | tf_op | source)
XLA Modules:
  0.0 479.1 jit_solution(6231306002654439550)
XLA Ops:
  7.4 1.7 collective-permute-start.1
  9.1 2.0 broadcast_in_dim.39
  11.2 0.7 constant_dynamic-update-slice_fusion.15
  11.9 0.8 fusion.27
  12.6 0.8 fusion.26
  14.0 4.2 collective-permute-start.3
  18.2 0.7 constant_dynamic-update-slice_fusion.14
  19.6 2.3 collective-permute-done.2
  21.8 1.8 collective-permute-start.5
  25.0 2.3 collective-permute-done.4
  27.3 1.9 collective-permute-start.7
  30.6 2.3 collective-permute-done.6
  32.8 3.0 collective-permute-start.9
  37.2 2.3 collective-permute-done.8
  39.5 3.0 collective-permute-start.11
  43.2 0.7 constant_dynamic-update-slice_fusion.5
  43.9 2.3 collective-permute-done.10
  46.1 3.1 collective-permute-start.13
  49.9 0.7 constant_dynamic-update-slice_fusion.3
  50.6 2.3 collective-permute-done.12
  52.9 0.7 constant_dynamic-update-slice_fusion.2
  54.3 5.6 %collective-permute-done.14 = bf16[128,896]{1,0:T(8,128)(2,1)S(1)} collective-permute-done((bf16[128,896]{1,0:T(8,128)(2,1)S(1)}, bf16[128,896]{1,0:T(8,128)(2,1)S(1)}, u32[]{:S(2)}, u32[]{:S(2)}) %collective-permute-start.14) | collective-permute-done | bytes 229408 | tf_op jit(solution)/shard_map/ppermute | solution.py:18
  60.6 38.6 %all-gather.2.cloned.1.call-done = bf16[2048,512]{1,0:T(8,128)(2,1)} async-done(((bf16[64,512]{1,0:T(8,128)(2,1)}), bf16[2048,512]{1,0:T(8,128)(2,1)}) %all-gather.2.cloned.1.call-update) | async-done | bytes 2097168 | tf_op jit(solution)/shard_map/all_gather | solution.py:89
  99.2 4.8 fusion.28
  104.0 2.3 convolution_bitcast_fusion
  106.3 2.3 convolution_bitcast_fusion.1
  108.6 110.0 %all-reduce.4.cloned.1.call-done = (f32[10,10]{1,0:T(8,128)}, f32[10,896]{0,1:T(8,128)}, f32[10,896]{1,0:T(8,128)}, f32[10,10]{1,0:T(8,128)}) async-done(((f32[10,10]{1,0:T(8,128)}, f32[10,896]{0,1:T(8,128)}, f32[10,896]{1,0:T(8,128)}, f32[10,10]{1,0:T(8,128)}), (f32[10,10]{1,0:T(8,128)}, f32[10,896]{0,1:T(8,128)}, f32[10,896]{1,0:T(8,128)}, f32[10,10]{1,0:T(8,128)})) %all-reduce.4.cloned.1.call-update) | async-done | bytes 72496 | tf_op jit(solution)/shard_map/psum | solution.py:94
  218.7 1.3 slice.532
  220.0 0.8 fusion.8
  220.7 0.7 fusion.22
  221.5 0.7 fusion.21
  222.9 1.3 slice.533
  224.2 1.4 gather_fusion
  226.9 34.4 %subtract_divide_fusion.9 = (f32[1,10]{1,0:T(1,128)S(1)}, f32[1,10]{1,0:T(1,128)S(1)}, f32[1,10]{1,0:T(1,128)S(1)}, f32[1,10]{1,0:T(1,128)S(1)}, f32[1,10]{1,0:T...) fusion(f32[10,10]{1,0:T(8,128)S(1)} %fusion.9, ...), kind=kLoop, calls=%fused_computation.52 | loop fusion | flops 1000 | bytes 1020 | tf_op jit(solution)/shard_map/div | solution.py:38
  261.4 1.5 fusion.29
  262.9 1.1 convolution_subtract_fusion.1
  264.3 1.6 fusion.31
  265.9 1.9 multiply_subtract_fusion
  267.8 3.3 fusion.32
  271.1 3.1 fusion.34
  274.2 149.3 %all-reduce = (f32[512,10]{1,0:T(8,128)S(1)}, f32[10,10]{1,0:T(8,128)S(1)}, f32[512,10]{1,0:T(8,128)S(1)}, f32[10,10]{1,0:T(8,128)S(1)}) all-reduce(f32[512,10]{1,0:T(8,128)S(1)} %fusion.32, f32[10,10]{1,0:T(8,128)S(1)} %fusion.24, f32[512,10]{1,0:T(8,128)S(1)} %fusion.34, ...), channel_id=1, replica_groups=mesh['row'=16,'col'=32] {'col'}, use_global_device_ids=true, to_apply=%region_6.7 | all-reduce | flops 10440 | bytes 83520 | tf_op jit(solution)/shard_map/psum | solution.py:106
  424.3 0.7 fusion.18
  425.0 0.7 fusion.19
  425.7 0.7 fusion.20
  429.2 34.2 %subtract_divide_fusion = (f32[1,10]{1,0:T(1,128)S(1)}, f32[1,10]{1,0:T(1,128)S(1)}, f32[1,10]{1,0:T(1,128)S(1)}, f32[1,10]{1,0:T(1,128)S(1)}, f32[1,10]{1,0:T(1...) fusion(f32[10,10]{1,0:T(8,128)S(1)} %fusion.9, ...), kind=kLoop, calls=%fused_computation.43 | loop fusion | flops 1000 | bytes 1020 | tf_op jit(solution)/shard_map/div | solution.py:38
  464.8 1.6 fusion.36
  466.4 3.1 fusion
  469.5 2.7 copy.12
  (61 shorter events, 13.5 us)
Async XLA Ops:
  6.5 6.9 %copy-start = (f32[10,896]{1,0:T(8,128)S(1)}, f32[10,896]{1,0:T(8,128)}, u32[]{:S(2)}) copy-start(f32[10,896]{1,0:T(8,128)} %param.11) | copy-start | bytes 107524
  6.5 4.6 copy-start.6
  6.5 5.3 %copy-start.3 = (f32[10,512]{1,0:T(8,128)S(1)}, f32[10,512]{1,0:T(8,128)}, u32[]{:S(2)}) copy-start(f32[10,512]{1,0:T(8,128)} %param.9) | copy-start | bytes 61444
  6.5 6.1 %copy-start.5 = (f32[10,512]{1,0:T(8,128)S(1)}, f32[10,512]{1,0:T(8,128)}, u32[]{:S(2)}) copy-start(f32[10,512]{1,0:T(8,128)} %param.8) | copy-start | bytes 61444
  6.5 7.2 %copy-start.4 = (f32[10,896]{1,0:T(8,128)S(1)}, f32[10,896]{1,0:T(8,128)}, u32[]{:S(2)}) copy-start(f32[10,896]{1,0:T(8,128)} %param.10) | copy-start | bytes 107524
  6.5 92.7 %all-gather.2.cloned.1.call-start = ((), (), s32[]{:S(2)}) async-start(), calls=%async_computation | async-start | bytes 2162688 | tf_op jit(solution)/shard_map/all_gather | solution.py:89
  7.3 211.4 %all-reduce.4.cloned.1.call-start = ((), (), s32[]{:S(2)}) async-start(), calls=%async_computation.1 | async-start | bytes 1064960 | tf_op jit(solution)/shard_map/psum | solution.py:94
  7.3 6.6 %collective-permute-start = (bf16[128,896]{1,0:T(8,128)(2,1)}, bf16[128,896]{1,0:T(8,128)(2,1)S(1)}, u32[]{:S(2)}, u32[]{:S(2)}) collective-permute-start(bf16[128,896]{1,0:T(8,128)(2,1)} %param.7), channel_id=1, source_target_pairs={{0,32},{32,64},{64,96},{96,128},{128,160},{160,192},{192,224},{224... | collective-permute-start | bytes 688136 | tf_op jit(solution)/shard_map/ppermute | solution.py:18
  7.4 6.6 %collective-permute-start.1 = (bf16[128,896]{1,0:T(8,128)(2,1)}, bf16[128,896]{1,0:T(8,128)(2,1)S(1)}, u32[]{:S(2)}, u32[]{:S(2)}) collective-permute-start(bf16[128,896]{1,0:T(8,128)(2,1)} %param.7), channel_id=1, source_target_pairs={{0,480},{32,0},{64,32},{96,64},{128,96},{160,128},{192,160},{224,1... | collective-permute-start | bytes 688136 | tf_op jit(solution)/shard_map/ppermute | solution.py:23
  13.9 7.9 %collective-permute-start.2 = (bf16[128,896]{1,0:T(8,128)(2,1)S(1)}, bf16[128,896]{1,0:T(8,128)(2,1)S(1)}, u32[]{:S(2)}, u32[]{:S(2)}) collective-permute-start(bf16[128,896]{1,0:T(8,128)(2,1)S(1)} %collective-permute-done), channel_id=1, source_target_pairs={{0,32},{32,64},{64,96},{96,128},{128,160},{160,192},{192,224},{224... | collective-permute-start | bytes 688136 | tf_op jit(solution)/shard_map/ppermute | solution.py:18
  14.0 7.9 %collective-permute-start.3 = (bf16[128,896]{1,0:T(8,128)(2,1)S(1)}, bf16[128,896]{1,0:T(8,128)(2,1)S(1)}, u32[]{:S(2)}, u32[]{:S(2)}) collective-permute-start(bf16[128,896]{1,0:T(8,128)(2,1)S(1)} %collective-permute-done.1), channel_id=1, source_target_pairs={{0,480},{32,0},{64,32},{96,64},{128,96},{160,128},{192,160},{224,1... | collective-permute-start | bytes 688136 | tf_op jit(solution)/shard_map/ppermute | solution.py:23
  21.8 5.4 %collective-permute-start.4 = (bf16[128,896]{1,0:T(8,128)(2,1)S(1)}, bf16[128,896]{1,0:T(8,128)(2,1)S(1)}, u32[]{:S(2)}, u32[]{:S(2)}) collective-permute-start(bf16[128,896]{1,0:T(8,128)(2,1)S(1)} %collective-permute-done.2), channel_id=1, source_target_pairs={{0,32},{32,64},{64,96},{96,128},{128,160},{160,192},{192,224},{224... | collective-permute-start | bytes 688136 | tf_op jit(solution)/shard_map/ppermute | solution.py:18
  21.8 5.4 %collective-permute-start.5 = (bf16[128,896]{1,0:T(8,128)(2,1)S(1)}, bf16[128,896]{1,0:T(8,128)(2,1)S(1)}, u32[]{:S(2)}, u32[]{:S(2)}) collective-permute-start(bf16[128,896]{1,0:T(8,128)(2,1)S(1)} %collective-permute-done.3), channel_id=1, source_target_pairs={{0,480},{32,0},{64,32},{96,64},{128,96},{160,128},{192,160},{224,1... | collective-permute-start | bytes 688136 | tf_op jit(solution)/shard_map/ppermute | solution.py:23
  27.3 5.6 %collective-permute-start.6 = (bf16[128,896]{1,0:T(8,128)(2,1)S(1)}, bf16[128,896]{1,0:T(8,128)(2,1)S(1)}, u32[]{:S(2)}, u32[]{:S(2)}) collective-permute-start(bf16[128,896]{1,0:T(8,128)(2,1)S(1)} %collective-permute-done.4), channel_id=1, source_target_pairs={{0,32},{32,64},{64,96},{96,128},{128,160},{160,192},{192,224},{224... | collective-permute-start | bytes 688136 | tf_op jit(solution)/shard_map/ppermute | solution.py:18
  27.3 5.6 %collective-permute-start.7 = (bf16[128,896]{1,0:T(8,128)(2,1)S(1)}, bf16[128,896]{1,0:T(8,128)(2,1)S(1)}, u32[]{:S(2)}, u32[]{:S(2)}) collective-permute-start(bf16[128,896]{1,0:T(8,128)(2,1)S(1)} %collective-permute-done.5), channel_id=1, source_target_pairs={{0,480},{32,0},{64,32},{96,64},{128,96},{160,128},{192,160},{224,1... | collective-permute-start | bytes 688136 | tf_op jit(solution)/shard_map/ppermute | solution.py:23
  32.8 6.6 %collective-permute-start.8 = (bf16[128,896]{1,0:T(8,128)(2,1)S(1)}, bf16[128,896]{1,0:T(8,128)(2,1)S(1)}, u32[]{:S(2)}, u32[]{:S(2)}) collective-permute-start(bf16[128,896]{1,0:T(8,128)(2,1)S(1)} %collective-permute-done.6), channel_id=1, source_target_pairs={{0,32},{32,64},{64,96},{96,128},{128,160},{160,192},{192,224},{224... | collective-permute-start | bytes 688136 | tf_op jit(solution)/shard_map/ppermute | solution.py:18
  32.8 6.6 %collective-permute-start.9 = (bf16[128,896]{1,0:T(8,128)(2,1)S(1)}, bf16[128,896]{1,0:T(8,128)(2,1)S(1)}, u32[]{:S(2)}, u32[]{:S(2)}) collective-permute-start(bf16[128,896]{1,0:T(8,128)(2,1)S(1)} %collective-permute-done.7), channel_id=1, source_target_pairs={{0,480},{32,0},{64,32},{96,64},{128,96},{160,128},{192,160},{224,1... | collective-permute-start | bytes 688136 | tf_op jit(solution)/shard_map/ppermute | solution.py:23
  39.5 6.7 %collective-permute-start.10 = (bf16[128,896]{1,0:T(8,128)(2,1)S(1)}, bf16[128,896]{1,0:T(8,128)(2,1)S(1)}, u32[]{:S(2)}, u32[]{:S(2)}) collective-permute-start(bf16[128,896]{1,0:T(8,128)(2,1)S(1)} %collective-permute-done.8), channel_id=1, source_target_pairs={{0,32},{32,64},{64,96},{96,128},{128,160},{160,192},{192,224},{224... | collective-permute-start | bytes 688136 | tf_op jit(solution)/shard_map/ppermute | solution.py:18
  39.5 6.7 %collective-permute-start.11 = (bf16[128,896]{1,0:T(8,128)(2,1)S(1)}, bf16[128,896]{1,0:T(8,128)(2,1)S(1)}, u32[]{:S(2)}, u32[]{:S(2)}) collective-permute-start(bf16[128,896]{1,0:T(8,128)(2,1)S(1)} %collective-permute-done.9), channel_id=1, source_target_pairs={{0,480},{32,0},{64,32},{96,64},{128,96},{160,128},{192,160},{224,1... | collective-permute-start | bytes 688136 | tf_op jit(solution)/shard_map/ppermute | solution.py:23
  46.1 6.8 %collective-permute-start.12 = (bf16[128,896]{1,0:T(8,128)(2,1)S(1)}, bf16[128,896]{1,0:T(8,128)(2,1)S(1)}, u32[]{:S(2)}, u32[]{:S(2)}) collective-permute-start(bf16[128,896]{1,0:T(8,128)(2,1)S(1)} %collective-permute-done.10), channel_id=1, source_target_pairs={{0,32},{32,64},{64,96},{96,128},{128,160},{160,192},{192,224},{224... | collective-permute-start | bytes 688136 | tf_op jit(solution)/shard_map/ppermute | solution.py:18
  46.1 7.5 %collective-permute-start.13 = (bf16[128,896]{1,0:T(8,128)(2,1)S(1)}, bf16[128,896]{1,0:T(8,128)(2,1)S(1)}, u32[]{:S(2)}, u32[]{:S(2)}) collective-permute-start(bf16[128,896]{1,0:T(8,128)(2,1)S(1)} %collective-permute-done.11), channel_id=1, source_target_pairs={{0,480},{32,0},{64,32},{96,64},{128,96},{160,128},{192,160},{224,1... | collective-permute-start | bytes 688136 | tf_op jit(solution)/shard_map/ppermute | solution.py:23
  52.9 7.0 %collective-permute-start.14 = (bf16[128,896]{1,0:T(8,128)(2,1)S(1)}, bf16[128,896]{1,0:T(8,128)(2,1)S(1)}, u32[]{:S(2)}, u32[]{:S(2)}) collective-permute-start(bf16[128,896]{1,0:T(8,128)(2,1)S(1)} %collective-permute-done.12), channel_id=1, source_target_pairs={{0,32},{32,64},{64,96},{96,128},{128,160},{160,192},{192,224},{224... | collective-permute-start | bytes 688136 | tf_op jit(solution)/shard_map/ppermute | solution.py:18
  267.8 3.3 copy-start.1
  274.2 192.2 %copy-start.2 = (f32[896,512]{1,0:T(8,128)S(1)}, f32[896,512]{1,0:T(8,128)}, u32[]{:S(2)}) copy-start(f32[896,512]{1,0:T(8,128)} %copy-done.1) | copy-start | bytes 5505028
Sparse Core Ops, SparseCore 0:
  10.5 88.6 all-gather.1
  108.7 109.8 all-reduce.3
